TPU v7x, 32 devices: a whole 2x2x4 slice. The times are simulated.
32 devices in a mesh: shard: 8 (over z, x), rep: 4 (over y, core).
Axes of the slice: x: 2, y: 2, z: 4, core: 2. Of those that a mesh axis runs over, the one named last changes fastest.
Arguments:
- images: bfloat16 [32, 197, 768], P(('shard', 'rep')), may hold values from -6 to 6
- cotangent: bfloat16 [32, 197, 768], P(('shard', 'rep')), may hold values from -6 to 6
- weights_in: float32 [768, 6144], P('shard'), may hold values from -13 to 13
- weights_down: float32 [3072, 768], P('shard'), may hold values from -0.109375 to 0.109375
- vectors: float32 [12, 768], P(None, 'shard'), may hold values from -1.5 to 1.5, as said below
- mean_in: float32 [768, 6144], P('shard'), may hold values from -256 to 256
- mean_down: float32 [3072, 768], P('shard'), may hold values from -256 to 256
- mean_vectors: float32 [12, 768], P(None, 'shard'), may hold values from -256 to 256
- square_in: float32 [768, 6144], P('shard'), may hold values from 63.04 to 6304
- square_down: float32 [3072, 768], P('shard'), may hold values from 63.04 to 6304
- square_vectors: float32 [12, 768], P(None, 'shard'), may hold values from 63.04 to 6304
Outputs:
- block_out: bfloat16 [32, 197, 768], P(('shard', 'rep'))
- input_grad: float32 [32, 197, 768], P(('shard', 'rep'))
- grad_in: float32 [768, 6144], P('shard')
- grad_down: float32 [3072, 768], P('shard')
- grad_vectors: float32 [12, 768], P(None, 'shard')
- updated_in: float32 [768, 6144], P('shard')
- updated_down: float32 [3072, 768], P('shard')
- updated_vectors: float32 [12, 768], P(None, 'shard')
- next_mean_in: float32 [768, 6144], P('shard')
- next_mean_down: float32 [3072, 768], P('shard')
- next_mean_vectors: float32 [12, 768], P(None, 'shard')
- next_square_in: float32 [768, 6144], P('shard')
- next_square_down: float32 [3072, 768], P('shard')
- next_square_vectors: float32 [12, 768], P(None, 'shard')
Inputs may be any that keep to these rules, and one draw needn't show every extreme that they name: `vectors`: rows 0 and 5 are the norms' gains.
All inputs are finite; a program needn't handle non-finite values.
Results may differ from a plain program's by a relative error of at most 0.023.
Values may be sent and summed in bfloat16 or wider, within the bound.
A program may use at most 128 MiB of HBM per device.

v0:
```python
import math
import jax
import jax.numpy as jnp
from jax import lax
from jax.sharding import PartitionSpec as P

HEADS = 12
NORM_EPS = 1e-06
BETA_ONE = 0.9
BETA_TWO = 0.95
ADAM_EPS = 1e-08
RATE_MATRIX = 0.008
RATE_VECTOR = 0.15
DECAY_MATRIX = 0.05
STEP_COUNT = 2.0


def to_half(array_in):
    return array_in.astype(jnp.bfloat16)


def matmul(left, right):
    return jnp.dot(left, right, preferred_element_type=jnp.float32)


def times_transposed(left, right):
    return lax.dot_general(
        left, right, (((1,), (1,)), ((), ())), preferred_element_type=jnp.float32
    )


def transposed_times(left, right):
    return lax.dot_general(
        left, right, (((0,), (0,)), ((), ())), preferred_element_type=jnp.float32
    )


def layer_norm(inputs, gain, shift):
    centred = inputs - jnp.mean(inputs, axis=-1, keepdims=True)
    inv_std = lax.rsqrt(jnp.mean(centred * centred, axis=-1, keepdims=True) + NORM_EPS)
    normed = centred * inv_std
    return (normed, inv_std, normed * gain + shift)


def norm_back(grad_after, normed, inv_std, gain):
    grad_normed = grad_after * gain
    grad_inputs = inv_std * (
        grad_normed
        - jnp.mean(grad_normed, axis=-1, keepdims=True)
        - normed * jnp.mean(grad_normed * normed, axis=-1, keepdims=True)
    )
    return (grad_inputs, jnp.sum(grad_after * normed, axis=0), jnp.sum(grad_after, axis=0))


def gaussian_unit(hidden):
    cdf_part = 0.5 * (1.0 + jax.scipy.special.erf(hidden * 0.7071067811865476))
    slope = cdf_part + hidden * jnp.exp(-0.5 * hidden * hidden) * 0.3989422804014327
    return (hidden * cdf_part, slope)


def head_scores(query_heads, key_heads, score_scale):
    return (
        jnp.einsum("bqhe,bkhe->bhqk", query_heads, key_heads, preferred_element_type=jnp.float32)
        * score_scale
    )


def forward_pass(images, matrix_half, down_half, vector_half):
    img_count, seq_len, model_width = images.shape
    head_dim = model_width // HEADS
    score_scale = 1.0 / math.sqrt(head_dim)
    row_count = img_count * seq_len
    head_shape = (img_count, seq_len, HEADS, head_dim)
    vector_float = vector_half.astype(jnp.float32)
    flat_in = images.reshape(row_count, model_width).astype(jnp.float32)
    normed_one, inv_one, pre_one = layer_norm(flat_in, vector_float[0], vector_float[1])
    act_one = to_half(pre_one)
    projected = matmul(act_one, matrix_half[:, : 3 * model_width])
    query_heads = to_half(projected[:, :model_width] + vector_float[2]).reshape(head_shape)
    key_heads = to_half(projected[:, model_width : 2 * model_width]).reshape(head_shape)
    value_heads = to_half(projected[:, 2 * model_width :] + vector_float[3]).reshape(head_shape)
    scores = head_scores(query_heads, key_heads, score_scale)
    log_total = jax.nn.logsumexp(scores, axis=-1, keepdims=True)
    probs_half = to_half(jnp.exp(scores - log_total))
    attended = to_half(
        jnp.einsum(
            "bhqk,bkhe->bqhe", probs_half, value_heads, preferred_element_type=jnp.float32
        ).reshape(row_count, model_width)
    )
    hidden_one = (
        flat_in
        + matmul(attended, matrix_half[:, 3 * model_width : 4 * model_width])
        + vector_float[4]
    )
    normed_two, inv_two, pre_two = layer_norm(hidden_one, vector_float[5], vector_float[6])
    act_two = to_half(pre_two)
    up_input = matmul(act_two, matrix_half[:, 4 * model_width :]) + vector_float[8:].reshape(-1)
    gelu_out, gelu_slope = gaussian_unit(up_input)
    gelu_half = to_half(gelu_out)
    block_out = to_half(hidden_one + matmul(gelu_half, down_half) + vector_float[7])
    saved = (
        normed_one,
        inv_one,
        act_one,
        query_heads,
        key_heads,
        value_heads,
        log_total,
        attended,
        normed_two,
        inv_two,
        act_two,
        gelu_slope,
        gelu_half,
    )
    return (block_out.reshape(images.shape), saved)


def backward_pass(cotangent, saved, matrix_half, down_half, vector_half):
    (
        normed_one,
        inv_one,
        act_one,
        query_heads,
        key_heads,
        value_heads,
        log_total,
        attended,
        normed_two,
        inv_two,
        act_two,
        gelu_slope,
        gelu_half,
    ) = saved
    img_count, seq_len, model_width = cotangent.shape
    head_dim = model_width // HEADS
    score_scale = 1.0 / math.sqrt(head_dim)
    row_count = img_count * seq_len
    head_shape = (img_count, seq_len, HEADS, head_dim)
    vector_float = vector_half.astype(jnp.float32)
    joint_weights = matrix_half[:, : 3 * model_width]
    output_weights = matrix_half[:, 3 * model_width : 4 * model_width]
    upward_weights = matrix_half[:, 4 * model_width :]
    grad_half = cotangent.reshape(row_count, model_width)
    grad_out = grad_half.astype(jnp.float32)
    grad_up = times_transposed(grad_half, down_half) * gelu_slope
    up_half = to_half(grad_up)
    grad_act_two = times_transposed(up_half, upward_weights)
    grad_norm_two, grad_gain_two, grad_shift_two = norm_back(
        grad_act_two, normed_two, inv_two, vector_float[5]
    )
    grad_hidden = grad_out + grad_norm_two
    hidden_half = to_half(grad_hidden)
    grad_att = to_half(times_transposed(hidden_half, output_weights)).reshape(head_shape)
    prob_float = jnp.exp(head_scores(query_heads, key_heads, score_scale) - log_total)
    probs_half = to_half(prob_float)
    grad_probs = jnp.einsum(
        "bqhe,bkhe->bhqk", grad_att, value_heads, preferred_element_type=jnp.float32
    )
    row_inner = jnp.sum(prob_float * grad_probs, axis=-1, keepdims=True)
    grad_scores = to_half(prob_float * (grad_probs - row_inner) * score_scale)
    grad_query = jnp.einsum(
        "bhqk,bkhe->bqhe", grad_scores, key_heads, preferred_element_type=jnp.float32
    ).reshape(row_count, model_width)
    grad_key = jnp.einsum(
        "bhqk,bqhe->bkhe", grad_scores, query_heads, preferred_element_type=jnp.float32
    ).reshape(row_count, model_width)
    grad_value = jnp.einsum(
        "bhqk,bqhe->bkhe", probs_half, grad_att, preferred_element_type=jnp.float32
    ).reshape(row_count, model_width)
    grad_proj = to_half(jnp.concatenate([grad_query, grad_key, grad_value], axis=1))
    grad_act_one = times_transposed(grad_proj, joint_weights)
    grad_norm_one, grad_gain_one, grad_shift_one = norm_back(
        grad_act_one, normed_one, inv_one, vector_float[0]
    )
    input_grad = (grad_hidden + grad_norm_one).reshape(cotangent.shape)
    grad_down = transposed_times(gelu_half, grad_half)
    small_rows = jnp.stack(
        [
            grad_gain_one,
            grad_shift_one,
            jnp.sum(grad_query, axis=0),
            jnp.sum(grad_value, axis=0),
            jnp.sum(grad_hidden, axis=0),
            grad_gain_two,
            grad_shift_two,
            jnp.sum(grad_out, axis=0),
        ]
    )
    grad_vectors = jnp.concatenate(
        [small_rows, jnp.sum(grad_up, axis=0).reshape(4, model_width)], axis=0
    )
    factors = (act_one, grad_proj, attended, hidden_half, act_two, up_half)
    return (input_grad, grad_down, grad_vectors, factors)


def adam_update(weights, first, second, gradient, rate, decay):
    next_first = BETA_ONE * first + (1.0 - BETA_ONE) * gradient
    next_second = BETA_TWO * second + (1.0 - BETA_TWO) * gradient * gradient
    corr_first = next_first / (1.0 - BETA_ONE**STEP_COUNT)
    corr_second = next_second / (1.0 - BETA_TWO**STEP_COUNT)
    updated = weights - rate * (corr_first / (jnp.sqrt(corr_second) + ADAM_EPS) + decay * weights)
    return (updated, next_first, next_second)


def local(
    images,
    cotangent,
    weights_in,
    weights_down,
    vectors,
    mean_in,
    mean_down,
    mean_vectors,
    square_in,
    square_down,
    square_vectors,
):
    halves = (to_half(weights_in), to_half(weights_down), to_half(vectors))
    forward_set = (
        lax.all_gather(halves[0], "shard", axis=0, tiled=True),
        lax.all_gather(halves[1], "shard", axis=0, tiled=True),
        lax.all_gather(halves[2], "shard", axis=1, tiled=True),
    )
    block_out, saved = forward_pass(images, forward_set[0], forward_set[1], forward_set[2])
    backward_set = (
        lax.all_gather(halves[0], "shard", axis=0, tiled=True),
        lax.all_gather(halves[1], "shard", axis=0, tiled=True),
        lax.all_gather(halves[2], "shard", axis=1, tiled=True),
    )
    input_grad, grad_down_local, grad_vectors_local, factors = backward_pass(
        cotangent, saved, backward_set[0], backward_set[1], backward_set[2]
    )
    act_one, grad_proj, attended, hidden_half, act_two, up_half = factors

    def column_part(activation, gradient):
        return transposed_times(activation, gradient)

    owned_in = lax.psum_scatter(
        jnp.concatenate(
            [
                column_part(act_one, grad_proj),
                column_part(attended, hidden_half),
                column_part(act_two, up_half),
            ],
            axis=1,
        ).astype(jnp.bfloat16),
        "shard",
        scatter_dimension=0,
        tiled=True,
    )
    owned_down, owned_vectors = (
        lax.psum_scatter(
            grad_down_local.astype(jnp.bfloat16), "shard", scatter_dimension=0, tiled=True
        ).astype(jnp.float32),
        lax.psum_scatter(
            grad_vectors_local.astype(jnp.bfloat16), "shard", scatter_dimension=1, tiled=True
        ).astype(jnp.float32),
    )
    grad_in, grad_down, grad_vectors = (
        lax.psum(owned_in, "rep").astype(jnp.float32),
        lax.psum(owned_down.astype(jnp.bfloat16), "rep").astype(jnp.float32),
        lax.psum(owned_vectors.astype(jnp.bfloat16), "rep").astype(jnp.float32),
    )
    new_in = adam_update(weights_in, mean_in, square_in, grad_in, RATE_MATRIX, DECAY_MATRIX)
    new_down = adam_update(
        weights_down, mean_down, square_down, grad_down, RATE_MATRIX, DECAY_MATRIX
    )
    new_vectors = adam_update(vectors, mean_vectors, square_vectors, grad_vectors, RATE_VECTOR, 0.0)
    return (
        block_out,
        input_grad,
        grad_in,
        grad_down,
        grad_vectors,
        new_in[0],
        new_down[0],
        new_vectors[0],
        new_in[1],
        new_down[1],
        new_vectors[1],
        new_in[2],
        new_down[2],
        new_vectors[2],
    )


def solution(mesh):
    placed = (
        P(("shard", "rep"), None, None),
        P(("shard", "rep"), None, None),
        P("shard", None),
        P("shard", None),
        P(None, "shard"),
        P("shard", None),
        P("shard", None),
        P(None, "shard"),
        P("shard", None),
        P("shard", None),
        P(None, "shard"),
    )
    return jax.shard_map(
        local,
        mesh=mesh,
        in_specs=placed,
        out_specs=(
            P(("shard", "rep"), None, None),
            P(("shard", "rep"), None, None),
            P("shard", None),
            P("shard", None),
            P(None, "shard"),
            P("shard", None),
            P("shard", None),
            P(None, "shard"),
            P("shard", None),
            P("shard", None),
            P(None, "shard"),
            P("shard", None),
            P("shard", None),
            P(None, "shard"),
        ),
        check_vma=False,
    )
```

profile of v0, /device:TPU:0, one launch (start us, length us, event | category | flops | bytes accessed | tf_op | source)
XLA Modules:
  0.0 623.4 jit_solution(6696602671923517766)
XLA Ops:
  7.2 2.9 convert_element_type.95
  10.2 0.0 all-gather.6.cloned.1.call-start
  10.2 0.9 convert_element_type.105
  11.2 33.3 %all-gather = bf16[8,96,12]{1,2,0:T(8,128)(2,1)S(1)} all-gather(bf16[1,96,12]{1,2,0:T(8,128)(2,1)S(1)} %convert_bitcast_fusion.1), channel_id=1, replica_groups=mesh['shard'=8,'rep'=4] {'shard'}, dimensions={0}, use_global_device_ids=true | all-gather | bytes 20736 | tf_op jit(solution)/shard_map/all_gather | solution.py:223
  44.5 0.1 reshape.207
  44.6 0.1 slice_reduce_fusion
  44.7 0.1 convert_reduce_fusion
  44.8 0.2 fusion.57
  45.1 105.8 %all-gather.4.cloned.1.call-done = bf16[768,6144]{1,0:T(8,128)(2,1)} async-done(((bf16[96,6144]{1,0:T(8,128)(2,1)}), bf16[768,6144]{1,0:T(8,128)(2,1)}) %all-gather.4.cloned.1.call-update) | async-done | bytes 9437200 | tf_op jit(solution)/shard_map/all_gather | solution.py:221
  150.9 3.0 fusion.10
  153.9 0.1 fusion.58
  154.0 0.9 copy.63
  154.9 0.2 copy.64
  155.1 0.2 copy.62
  155.3 1.5 multiply_reduce_fusion.1
  156.9 0.5 exponential_reduce_fusion
  157.4 0.6 convolution_convert_fusion.4
  158.0 2.0 fusion.87
  160.0 0.2 multiply_reduce_fusion.4
  160.3 5.4 multiply_convert_fusion.1
  165.7 1.0 copy-done.7
  166.7 3.7 convolution_convert_fusion
  170.4 0.2 reduce-scatter.6.cloned.1.call-start
  170.7 60.5 %all-gather.6.cloned.1.call-done = bf16[3072,768]{1,0:T(8,128)(2,1)} async-done(((bf16[384,768]{1,0:T(8,128)(2,1)}), bf16[3072,768]{1,0:T(8,128)(2,1)}) %all-gather.6.cloned.1.call-update) | async-done | bytes 4718608 | tf_op jit(solution)/shard_map/all_gather | solution.py:222
  231.2 5.0 fusion.90
  236.2 4.7 multiply_reduce_fusion.2
  240.9 1.4 fusion.84
  242.3 2.5 convolution_convert_fusion.5
  244.8 1.9 copy.66
  246.7 2.5 convolution_convert_fusion.3
  249.2 2.4 copy.70
  251.6 3.0 fusion.91
  254.6 4.7 fusion.30
  259.3 4.9 fusion.86
  264.2 0.7 fusion.85
  264.9 0.7 copy-done.23
  265.6 1.3 convolution_convert_fusion.2
  267.0 0.1 copy-done.21
  267.1 1.6 convolution_convert_fusion.1
  268.7 4.2 pad_maximum_fusion
  272.9 0.3 reduce-scatter.10.cloned.1.call-start
  273.2 0.7 copy-done.15
  273.9 0.1 reduce.9
  274.0 0.1 stack.35
  274.1 0.1 stack.34
  274.2 0.0 copy-done.29
  274.2 0.1 copy-done.31
  274.3 3.6 fusion.56
  277.9 0.1 concatenate.14
  278.0 0.8 copy.76
  278.9 50.0 %reduce-scatter.8.cloned.1.call-done = bf16[384,768]{1,0:T(8,128)(2,1)} async-done(((bf16[3072,768]{1,0:T(8,128)(2,1)}), bf16[384,768]{1,0:T(8,128)(2,1)}) %reduce-scatter.8.cloned.1.call-update) | async-done | bytes 589840 | tf_op jit(solution)/shard_map/reduce_scatter | solution.py:253
  328.9 165.2 %reduce-scatter.6.cloned.1.call-done = bf16[96,6144]{1,0:T(8,128)(2,1)} async-done(((bf16[768,6144]{1,0:T(8,128)(2,1)}), bf16[96,6144]{1,0:T(8,128)(2,1)}) %reduce-scatter.6.cloned.1.call-update) | async-done | bytes 1179664 | tf_op jit(solution)/shard_map/reduce_scatter | solution.py:239
  494.2 0.3 fusion.55
  494.4 1.4 copy.71
  495.9 4.3 fusion.37
  500.2 58.6 %reduce-scatter.10.cloned.1.call-done = bf16[96,12]{1,0:T(8,128)(2,1)} async-done(((bf16[768,12]{1,0:T(8,128)(2,1)}), bf16[96,12]{1,0:T(8,128)(2,1)}) %reduce-scatter.10.cloned.1.call-update) | async-done | bytes 2320
  558.8 0.8 copy.77
  559.6 5.7 psum.23
  565.3 0.6 multiply_subtract_fusion.2
  565.9 40.4 %all-reduce.3.cloned.1.call-done = (bf16[96,6144]{1,0:T(8,128)(2,1)}, bf16[384,768]{1,0:T(8,128)(2,1)}) async-done(((bf16[96,6144]{1,0:T(8,128)(2,1)}, bf16[384,768]{1,0:T(8,128)(2,1)}), (bf16[96,6144]{1,0:T(8,128)(2,1)}, bf16[384,768]{1,0:T(8,128)(2,1)})) %all-reduce.3.cloned.1.call-update) | async-done | bytes 1769488 | tf_op jit(solution)/shard_map/psum | solution.py:261
  606.3 4.6 multiply_subtract_fusion.1
  610.9 1.1 copy-done.17
  612.0 0.3 copy-done.22
  612.3 4.3 multiply_subtract_fusion
  (86 shorter events, 0.5 us)
Async XLA Ops:
  7.2 3.0 copy-start.3
  7.2 143.7 %all-gather.4.cloned.1.call-start = ((), (), s32[]{:S(2)}) async-start(), calls=%async_computation.3 | async-start | bytes 10616832 | tf_op jit(solution)/shard_map/all_gather | solution.py:221
  10.1 1.0 copy-start.25
  10.1 34.5 %copy-start.9 = (bf16[1,197,768]{2,1,0:T(8,128)(2,1)S(1)}, bf16[1,197,768]{2,1,0:T(8,128)(2,1)}, u32[]{:S(2)}) copy-start(bf16[1,197,768]{2,1,0:T(8,128)(2,1)} %param.11) | copy-start | bytes 907780
  10.2 221.0 %all-gather.6.cloned.1.call-start = ((), (), s32[]{:S(2)}) async-start(), calls=%async_computation.4 | async-start | bytes 5308416 | tf_op jit(solution)/shard_map/all_gather | solution.py:222
  11.1 317.8 %reduce-scatter.8.cloned.1.call-start = ((), (), s32[]{:S(2)}) async-start(), calls=%async_computation.6 | async-start | bytes 5308416 | tf_op jit(solution)/shard_map/reduce_scatter | solution.py:253
  155.1 2.2 copy-start.18
  156.8 1.1 copy-start.10
  158.0 2.3 copy-start.19
  160.0 76.2 %copy-start.1 = (f32[197,768]{1,0:T(8,128)}, f32[197,768]{1,0:T(8,128)S(1)}, u32[]{:S(2)}) copy-start(f32[197,768]{1,0:T(8,128)S(1)} %get-tuple-element.111) | copy-start | bytes 1815556
  160.3 6.4 %copy-start.13 = (bf16[1,197,768]{2,1,0:T(8,128)(2,1)S(1)}, bf16[1,197,768]{2,1,0:T(8,128)(2,1)}, u32[]{:S(2)}) copy-start(bf16[1,197,768]{2,1,0:T(8,128)(2,1)} %param.12) | copy-start | bytes 907780
  165.7 1.0 copy-start.7
  170.4 323.7 %reduce-scatter.6.cloned.1.call-start = ((), (), s32[]{:S(2)}) async-start(), calls=%async_computation.5 | async-start | bytes 10616832 | tf_op jit(solution)/shard_map/reduce_scatter | solution.py:239
  236.2 4.7 copy-start.20
  236.2 4.7 copy-start.14
  259.3 4.9 copy-start.6
  264.1 1.5 copy-start.11
  264.1 1.5 copy-start.28
  264.1 1.5 copy-start.30
  264.8 0.8 copy-start.23
  265.6 1.3 copy-start.2
  265.6 1.5 copy-start.21
  267.1 1.6 copy-start.5
  272.9 1.0 copy-start.15
  272.9 1.3 copy-start.12
  272.9 1.3 copy-start.24
  272.9 1.3 copy-start.29
  272.9 1.4 copy-start.31
  272.9 285.9 %reduce-scatter.10.cloned.1.call-start = ((), (), s32[]{:S(2)}) async-start(), calls=%async_computation.7 | async-start | bytes 221184
  278.9 327.5 %all-reduce.3.cloned.1.call-start = ((), (), s32[]{:S(2)}) async-start(), calls=%async_computation.8 | async-start | bytes 3538944 | tf_op jit(solution)/shard_map/psum | solution.py:261
  494.2 1.7 copy-start.8
  495.9 69.4 %copy-start.26 = (f32[12,96]{1,0:T(8,128)S(1)}, f32[12,96]{1,0:T(8,128)}, u32[]{:S(2)}) copy-start(f32[12,96]{1,0:T(8,128)} %param.18) | copy-start | bytes 13828
  495.9 69.4 %copy-start.27 = (f32[12,96]{1,0:T(8,128)S(1)}, f32[12,96]{1,0:T(8,128)}, u32[]{:S(2)}) copy-start(f32[12,96]{1,0:T(8,128)} %param.21) | copy-start | bytes 13828
  495.9 110.4 %copy-start.4 = (f32[384,768]{1,0:T(8,128)S(1)}, f32[384,768]{1,0:T(8,128)}, u32[]{:S(2)}) copy-start(f32[384,768]{1,0:T(8,128)} %param.14) | copy-start | bytes 3538948
  606.3 4.6 copy-start
  606.3 4.6 copy-start.16
  606.3 5.7 copy-start.17
  606.3 5.9 copy-start.22
Sparse Core Ops, SparseCore 0:
  10.8 140.0 all-gather.3
  153.6 77.5 all-gather.5
  234.9 94.0 reduce-scatter.7
  332.3 161.7 reduce-scatter.5
  497.8 60.9 reduce-scatter.9
  561.2 45.0 all-reduce.2
where the time goes:
time: 624 us; the launch traced here: 623 us
  waiting for transfers between devices  481 us (77%)
  matrix products  54.9 us (9%)
  blocking collectives  38.9 us (6%)
  other arithmetic  20.4 us (3%)
  between operations  14.6 us (2%)
  local copies, waits for them, and re-layouts  13.3 us (2%)
    reduce_scatter x1, waiting for transfers between devices, local(): lax.psum_scatter(jnp.concatenate([column_part(act_one, grad_proj), column...  165 us
    all_gather x1, waiting for transfers between devices, local(): lax.all_gather(halves[0], 'shard', axis=0, tiled=True)  106 us
    all_gather x1, waiting for transfers between devices, local(): lax.all_gather(halves[1], 'shard', axis=0, tiled=True)  60.5 us
    unnamed x7, waiting for transfers between devices  58.7 us
    reduce_scatter x1, waiting for transfers between devices, local(): lax.psum_scatter(grad_down_local.astype(jnp.bfloat16), 'shard', scatter_d...  50 us
    psum x1, waiting for transfers between devices, local(): lax.psum(owned_in, 'rep').astype(jnp.float32)  40.4 us
    all_gather x1, blocking collectives, local(): lax.all_gather(halves[2], 'shard', axis=1, tiled=True)  33.3 us
    dot_general x4, matrix products, times_transposed(): lax.dot_general(left, right, (((1,), (1,)), ((), ())), preferred_element_...  15.7 us
  transfers between devices with their start and end apart: 6, of which 6 were waited for; matrix products, arithmetic and copies ran while one was open for 12% of the time, Pallas kernels for 0%

commit v1 on v0

--- a/solution.py
+++ b/solution.py
@@ -216,10 +216,31 @@
     square_down,
     square_vectors,
 ):
+
+    def replace_target(k_dim, s0):
+        a_name = "shard"
+        before, x_new, small = (
+            jax.lax.psum(1, a_name),
+            jax.lax.axis_index(a_name),
+            s0.shape[k_dim],
+        )
+        by_place = [t * before if dev_i == k_dim else t for dev_i, t in enumerate(s0.shape)]
+        main = lax.dynamic_update_slice_in_dim(
+            jnp.zeros(by_place, s0.dtype), s0, x_new * small, axis=k_dim
+        )
+        for j0 in range(1, before):
+            s0 = jax.lax.ppermute(
+                s0, a_name, list(map(lambda dev_i: (dev_i, (dev_i + 1) % before), range(before)))
+            )
+            main = lax.dynamic_update_slice_in_dim(
+                main, s0, (x_new - j0) % before * small, axis=k_dim
+            )
+        return main
+
     halves = (to_half(weights_in), to_half(weights_down), to_half(vectors))
     forward_set = (
         lax.all_gather(halves[0], "shard", axis=0, tiled=True),
-        lax.all_gather(halves[1], "shard", axis=0, tiled=True),
+        replace_target(0, halves[1]),
         lax.all_gather(halves[2], "shard", axis=1, tiled=True),
     )
     block_out, saved = forward_pass(images, forward_set[0], forward_set[1], forward_set[2])

time: 624 us -> 706 us (1.13)
  waiting for transfers between devices: 481 us -> 548 us
  local copies, waits for them, and re-layouts: 13.3 us -> 23.8 us
    ppermute x0 -> x7, waiting for transfers between devices: none -> 101 us  [replace_target(): jax.lax.ppermute(s0, a_name, list(map(lambda dev_i: (dev_i, (dev_i + 1) %...]
    reduce_scatter x1, waiting for transfers between devices: 50 us -> 19.6 us  [local(): lax.psum_scatter(grad_down_local.astype(jnp.bfloat16), 'shard', scatter_d...]
    dynamic_update_slice x0 -> x7, local copies, waits for them, and re-layouts: none -> 8.26 us  [replace_target(): lax.dynamic_update_slice_in_dim(main, s0, (x_new - j0) % before * small,...]
  transfers between devices with their start and end apart: 6 -> 13, of which waited for: 6 -> 13; matrix products, arithmetic and copies ran while one was open for 12% -> 12% of each run, Pallas kernels for 0% -> 0%
where the time goes in v1:
time: 706 us; the launch traced here: 705 us
  waiting for transfers between devices  548 us (78%)
  matrix products  55 us (8%)
  blocking collectives  39.1 us (6%)
  local copies, waits for them, and re-layouts  23.8 us (3%)
  other arithmetic  21 us (3%)
  between operations  14.6 us (2%)
    reduce_scatter x1, waiting for transfers between devices, local(): lax.psum_scatter(jnp.concatenate([column_part(act_one, grad_proj), column...  165 us
    all_gather x1, waiting for transfers between devices, local(): lax.all_gather(halves[0], 'shard', axis=0, tiled=True)  102 us
    ppermute x7, waiting for transfers between devices, replace_target(): jax.lax.ppermute(s0, a_name, list(map(lambda dev_i: (dev_i, (dev_i + 1) %...  101 us
    all_gather x1, waiting for transfers between devices, local(): lax.all_gather(halves[1], 'shard', axis=0, tiled=True)  60.5 us
    unnamed x7, waiting for transfers between devices  58.8 us
    psum x1, waiting for transfers between devices, local(): lax.psum(owned_in, 'rep').astype(jnp.float32)  40.4 us
    all_gather x1, blocking collectives, local(): lax.all_gather(halves[2], 'shard', axis=1, tiled=True)  33.5 us
    reduce_scatter x1, waiting for transfers between devices, local(): lax.psum_scatter(grad_down_local.astype(jnp.bfloat16), 'shard', scatter_d...  19.6 us
  transfers between devices with their start and end apart: 13, of which 13 were waited for; matrix products, arithmetic and copies ran while one was open for 12% of the time, Pallas kernels for 0%

profile of v1, /device:TPU:0, one launch (start us, length us, event | category | flops | bytes accessed | tf_op | source)
XLA Modules:
  0.0 705.2 jit_solution(8236575403257058351)
XLA Ops:
  7.2 2.8 convert_element_type.95
  10.1 0.3 broadcast_in_dim.5
  10.4 0.9 copy-done.4
  11.3 0.9 constant_dynamic-update-slice_fusion.7
  12.2 2.2 copy-done.7
  14.6 33.5 %all-gather = bf16[8,96,12]{1,2,0:T(8,128)(2,1)S(1)} all-gather(bf16[1,96,12]{1,2,0:T(8,128)(2,1)S(1)} %convert_bitcast_fusion.1), channel_id=1, replica_groups=mesh['shard'=8,'rep'=4] {'shard'}, dimensions={0}, use_global_device_ids=true | all-gather | bytes 20736 | tf_op jit(solution)/shard_map/all_gather | solution.py:244
  48.4 0.2 fusion.57
  48.6 102.4 %all-gather.4.cloned.1.call-done = bf16[768,6144]{1,0:T(8,128)(2,1)} async-done(((bf16[96,6144]{1,0:T(8,128)(2,1)}), bf16[768,6144]{1,0:T(8,128)(2,1)}) %all-gather.4.cloned.1.call-update) | async-done | bytes 9437200 | tf_op jit(solution)/shard_map/all_gather | solution.py:242
  151.0 3.0 fusion.10
  154.3 0.9 copy.63
  155.4 1.7 multiply_reduce_fusion.1
  157.1 0.5 exponential_reduce_fusion
  157.6 0.6 convolution_convert_fusion.4
  158.2 2.0 fusion.87
  160.5 5.4 multiply_convert_fusion.1
  165.9 1.0 copy-done.9
  166.9 3.6 convolution_convert_fusion
  170.8 60.5 %all-gather.6.cloned.1.call-done = bf16[3072,768]{1,0:T(8,128)(2,1)} async-done(((bf16[384,768]{1,0:T(8,128)(2,1)}), bf16[3072,768]{1,0:T(8,128)(2,1)}) %all-gather.6.cloned.1.call-update) | async-done | bytes 4718608 | tf_op jit(solution)/shard_map/all_gather | solution.py:249
  231.3 5.0 fusion.90
  236.3 4.7 multiply_reduce_fusion.2
  241.0 1.4 fusion.84
  242.4 2.5 convolution_convert_fusion.5
  244.9 1.9 copy.66
  246.8 2.5 convolution_convert_fusion.3
  249.3 2.4 copy.70
  251.7 3.0 fusion.91
  254.7 4.7 fusion.30
  259.3 4.8 fusion.86
  264.2 0.7 fusion.85
  264.9 0.7 copy-done.26
  265.7 1.3 convolution_convert_fusion.2
  267.2 1.6 convolution_convert_fusion.1
  268.8 4.2 pad_maximum_fusion
  273.0 1.0 copy-done.18
  274.0 0.8 collective-permute-start
  274.8 21.0 %collective-permute-done = bf16[384,768]{1,0:T(8,128)(2,1)S(1)} collective-permute-done((bf16[384,768]{1,0:T(8,128)(2,1)S(1)}, bf16[384,768]{1,0:T(8,128)(2,1)S(1)}, u32[]{:S(2)}, u32[]{:S(2)}) %collective-permute-start) | collective-permute-done | bytes 589856 | tf_op jit(solution)/shard_map/ppermute | solution.py:232
  295.8 18.7 %collective-permute-done.1 = bf16[384,768]{1,0:T(8,128)(2,1)S(1)} collective-permute-done((bf16[384,768]{1,0:T(8,128)(2,1)S(1)}, bf16[384,768]{1,0:T(8,128)(2,1)S(1)}, u32[]{:S(2)}, u32[]{:S(2)}) %collective-permute-start.1) | collective-permute-done | bytes 589856 | tf_op jit(solution)/shard_map/ppermute | solution.py:232
  314.5 2.5 collective-permute-start.2
  316.9 13.4 %collective-permute-done.2 = bf16[384,768]{1,0:T(8,128)(2,1)S(1)} collective-permute-done((bf16[384,768]{1,0:T(8,128)(2,1)S(1)}, bf16[384,768]{1,0:T(8,128)(2,1)S(1)}, u32[]{:S(2)}, u32[]{:S(2)}) %collective-permute-start.2) | collective-permute-done | bytes 589856 | tf_op jit(solution)/shard_map/ppermute | solution.py:232
  330.3 15.0 %collective-permute-done.3 = bf16[384,768]{1,0:T(8,128)(2,1)S(1)} collective-permute-done((bf16[384,768]{1,0:T(8,128)(2,1)S(1)}, bf16[384,768]{1,0:T(8,128)(2,1)S(1)}, u32[]{:S(2)}, u32[]{:S(2)}) %collective-permute-start.3) | collective-permute-done | bytes 589856 | tf_op jit(solution)/shard_map/ppermute | solution.py:232
  345.3 14.2 %collective-permute-done.4 = bf16[384,768]{1,0:T(8,128)(2,1)} collective-permute-done((bf16[384,768]{1,0:T(8,128)(2,1)S(1)}, bf16[384,768]{1,0:T(8,128)(2,1)}, u32[]{:S(2)}, u32[]{:S(2)}) %collective-permute-start.4) | collective-permute-done | bytes 589856 | tf_op jit(solution)/shard_map/ppermute | solution.py:232
  359.6 0.9 constant_dynamic-update-slice_fusion.6
  360.5 12.6 %collective-permute-done.5 = bf16[384,768]{1,0:T(8,128)(2,1)} collective-permute-done((bf16[384,768]{1,0:T(8,128)(2,1)}, bf16[384,768]{1,0:T(8,128)(2,1)}, u32[]{:S(2)}, u32[]{:S(2)}) %collective-permute-start.5) | collective-permute-done | bytes 589856 | tf_op jit(solution)/shard_map/ppermute | solution.py:232
  373.1 0.9 constant_dynamic-update-slice_fusion.5
  374.0 0.9 constant_dynamic-update-slice_fusion.4
  374.9 0.9 constant_dynamic-update-slice_fusion.3
  375.7 2.0 constant_dynamic-update-slice_fusion.2
  377.7 2.0 constant_dynamic-update-slice_fusion.1
  379.7 6.2 collective-permute-done.6
  385.9 0.8 constant_dynamic-update-slice_fusion
  386.8 3.6 fusion.56
  390.7 0.8 copy.76
  391.6 19.6 %reduce-scatter.8.cloned.1.call-done = bf16[384,768]{1,0:T(8,128)(2,1)} async-done(((bf16[3072,768]{1,0:T(8,128)(2,1)}), bf16[384,768]{1,0:T(8,128)(2,1)}) %reduce-scatter.8.cloned.1.call-update) | async-done | bytes 589840 | tf_op jit(solution)/shard_map/reduce_scatter | solution.py:274
  411.1 165.2 %reduce-scatter.6.cloned.1.call-done = bf16[96,6144]{1,0:T(8,128)(2,1)} async-done(((bf16[768,6144]{1,0:T(8,128)(2,1)}), bf16[96,6144]{1,0:T(8,128)(2,1)}) %reduce-scatter.6.cloned.1.call-update) | async-done | bytes 1179664 | tf_op jit(solution)/shard_map/reduce_scatter | solution.py:260
  576.4 0.3 fusion.55
  576.7 1.4 copy.71
  578.1 4.4 fusion.37
  582.5 58.7 %reduce-scatter.10.cloned.1.call-done = bf16[96,12]{1,0:T(8,128)(2,1)} async-done(((bf16[768,12]{1,0:T(8,128)(2,1)}), bf16[96,12]{1,0:T(8,128)(2,1)}) %reduce-scatter.10.cloned.1.call-update) | async-done | bytes 2320
  641.2 0.8 copy.77
  642.0 5.7 psum.23
  647.7 0.6 multiply_subtract_fusion.2
  648.3 40.4 %all-reduce.3.cloned.1.call-done = (bf16[96,6144]{1,0:T(8,128)(2,1)}, bf16[384,768]{1,0:T(8,128)(2,1)}) async-done(((bf16[96,6144]{1,0:T(8,128)(2,1)}, bf16[384,768]{1,0:T(8,128)(2,1)}), (bf16[96,6144]{1,0:T(8,128)(2,1)}, bf16[384,768]{1,0:T(8,128)(2,1)})) %all-reduce.3.cloned.1.call-update) | async-done | bytes 1769488 | tf_op jit(solution)/shard_map/psum | solution.py:282
  688.7 7.2 %multiply_subtract_fusion = (f32[96,6144]{1,0:T(8,128)}, f32[96,6144]{1,0:T(8,128)}, f32[96,6144]{1,0:T(8,128)}, f32[96,6144]{1,0:T(8,128)}) fusion(f32[96,6144]{1,0:T(8,128)S(1)} %copy-done, f32[96,6144]{1,0:T(8,128)} %param.16, f32[96,6144]{1,0:T(8,128)} %param.19, bf16[96,6144]{1,0:T(8,128)(2,1)} %get-tuple-element.86), kind=kLoop, calls=%fused_computation.29 | loop fusion | flops 9437184 | bytes 17694720 | tf_op jit(solution)/shard_map/sub | solution.py:202
  695.9 2.4 multiply_subtract_fusion.1
  (114 shorter events, 2.2 us)
Async XLA Ops:
  7.2 143.8 %all-gather.4.cloned.1.call-start = ((), (), s32[]{:S(2)}) async-start(), calls=%async_computation.3 | async-start | bytes 10616832 | tf_op jit(solution)/shard_map/all_gather | solution.py:242
  10.1 1.3 copy-start.4
  10.1 221.2 %all-gather.6.cloned.1.call-start = ((), (), s32[]{:S(2)}) async-start(), calls=%async_computation.4 | async-start | bytes 5308416 | tf_op jit(solution)/shard_map/all_gather | solution.py:249
  11.3 3.2 copy-start.28
  11.3 36.9 %copy-start.11 = (bf16[1,197,768]{2,1,0:T(8,128)(2,1)S(1)}, bf16[1,197,768]{2,1,0:T(8,128)(2,1)}, u32[]{:S(2)}) copy-start(bf16[1,197,768]{2,1,0:T(8,128)(2,1)} %param.11) | copy-start | bytes 907780
  12.2 2.2 copy-start.7
  14.5 396.6 %reduce-scatter.8.cloned.1.call-start = ((), (), s32[]{:S(2)}) async-start(), calls=%async_computation.6 | async-start | bytes 5308416 | tf_op jit(solution)/shard_map/reduce_scatter | solution.py:274
  155.4 2.2 copy-start.19
  157.1 1.1 copy-start.12
  158.2 2.3 copy-start.20
  160.3 76.0 %copy-start.1 = (f32[197,768]{1,0:T(8,128)}, f32[197,768]{1,0:T(8,128)S(1)}, u32[]{:S(2)}) copy-start(f32[197,768]{1,0:T(8,128)S(1)} %get-tuple-element.113) | copy-start | bytes 1815556
  160.5 6.4 copy-start.15
  165.9 1.0 copy-start.9
  170.6 405.8 %reduce-scatter.6.cloned.1.call-start = ((), (), s32[]{:S(2)}) async-start(), calls=%async_computation.5 | async-start | bytes 10616832 | tf_op jit(solution)/shard_map/reduce_scatter | solution.py:260
  236.3 4.7 copy-start.21
  236.3 4.7 copy-start.16
  259.3 4.8 copy-start.8
  264.2 1.5 copy-start.13
  264.2 1.5 copy-start.31
  264.2 1.5 copy-start.33
  264.9 0.8 copy-start.26
  265.7 1.3 copy-start.2
  265.7 1.5 copy-start.22
  267.2 1.6 copy-start.6
  272.9 1.1 copy-start.18
  272.9 86.6 %copy-start.17 = (bf16[1,197,768]{2,1,0:T(8,128)(2,1)S(1)}, bf16[1,197,768]{2,1,0:T(8,128)(2,1)}, u32[]{:S(2)}) copy-start(bf16[1,197,768]{2,1,0:T(8,128)(2,1)} %param.12) | copy-start | bytes 907780
  273.0 368.2 %reduce-scatter.10.cloned.1.call-start = ((), (), s32[]{:S(2)}) async-start(), calls=%async_computation.7 | async-start | bytes 221184
  274.0 21.8 %collective-permute-start = (bf16[384,768]{1,0:T(8,128)(2,1)S(1)}, bf16[384,768]{1,0:T(8,128)(2,1)S(1)}, u32[]{:S(2)}, u32[]{:S(2)}) collective-permute-start(bf16[384,768]{1,0:T(8,128)(2,1)S(1)} %copy-done.18), channel_id=1, source_target_pairs={{0,4},{4,8},{8,12},{12,16},{16,20},{20,24},{24,28},{28,0},{1,5},{5... | collective-permute-start | bytes 1769480 | tf_op jit(solution)/shard_map/ppermute | solution.py:232
  295.8 18.7 %collective-permute-start.1 = (bf16[384,768]{1,0:T(8,128)(2,1)S(1)}, bf16[384,768]{1,0:T(8,128)(2,1)S(1)}, u32[]{:S(2)}, u32[]{:S(2)}) collective-permute-start(bf16[384,768]{1,0:T(8,128)(2,1)S(1)} %collective-permute-done), channel_id=1, source_target_pairs={{0,4},{4,8},{8,12},{12,16},{16,20},{20,24},{24,28},{28,0},{1,5},{5... | collective-permute-start | bytes 1769480 | tf_op jit(solution)/shard_map/ppermute | solution.py:232
  314.5 15.8 %collective-permute-start.2 = (bf16[384,768]{1,0:T(8,128)(2,1)S(1)}, bf16[384,768]{1,0:T(8,128)(2,1)S(1)}, u32[]{:S(2)}, u32[]{:S(2)}) collective-permute-start(bf16[384,768]{1,0:T(8,128)(2,1)S(1)} %collective-permute-done.1), channel_id=1, source_target_pairs={{0,4},{4,8},{8,12},{12,16},{16,20},{20,24},{24,28},{28,0},{1,5},{5... | collective-permute-start | bytes 1769480 | tf_op jit(solution)/shard_map/ppermute | solution.py:232
  330.3 15.0 %collective-permute-start.3 = (bf16[384,768]{1,0:T(8,128)(2,1)S(1)}, bf16[384,768]{1,0:T(8,128)(2,1)S(1)}, u32[]{:S(2)}, u32[]{:S(2)}) collective-permute-start(bf16[384,768]{1,0:T(8,128)(2,1)S(1)} %collective-permute-done.2), channel_id=1, source_target_pairs={{0,4},{4,8},{8,12},{12,16},{16,20},{20,24},{24,28},{28,0},{1,5},{5... | collective-permute-start | bytes 1769480 | tf_op jit(solution)/shard_map/ppermute | solution.py:232
  345.3 14.2 %collective-permute-start.4 = (bf16[384,768]{1,0:T(8,128)(2,1)S(1)}, bf16[384,768]{1,0:T(8,128)(2,1)}, u32[]{:S(2)}, u32[]{:S(2)}) collective-permute-start(bf16[384,768]{1,0:T(8,128)(2,1)S(1)} %collective-permute-done.3), channel_id=1, source_target_pairs={{0,4},{4,8},{8,12},{12,16},{16,20},{20,24},{24,28},{28,0},{1,5},{5... | collective-permute-start | bytes 1769480 | tf_op jit(solution)/shard_map/ppermute | solution.py:232
  359.5 13.6 %collective-permute-start.5 = (bf16[384,768]{1,0:T(8,128)(2,1)}, bf16[384,768]{1,0:T(8,128)(2,1)}, u32[]{:S(2)}, u32[]{:S(2)}) collective-permute-start(bf16[384,768]{1,0:T(8,128)(2,1)} %collective-permute-done.4), channel_id=1, source_target_pairs={{0,4},{4,8},{8,12},{12,16},{16,20},{20,24},{24,28},{28,0},{1,5},{5... | collective-permute-start | bytes 1769480 | tf_op jit(solution)/shard_map/ppermute | solution.py:232
  373.1 12.8 %collective-permute-start.6 = (bf16[384,768]{1,0:T(8,128)(2,1)}, bf16[384,768]{1,0:T(8,128)(2,1)S(1)}, u32[]{:S(2)}, u32[]{:S(2)}) collective-permute-start(bf16[384,768]{1,0:T(8,128)(2,1)} %collective-permute-done.5), channel_id=1, source_target_pairs={{0,4},{4,8},{8,12},{12,16},{16,20},{20,24},{24,28},{28,0},{1,5},{5... | collective-permute-start | bytes 1769480 | tf_op jit(solution)/shard_map/ppermute | solution.py:232
  374.9 11.9 %copy-start.14 = (bf16[1,197,768]{2,1,0:T(8,128)(2,1)S(1)}, bf16[1,197,768]{2,1,0:T(8,128)(2,1)}, u32[]{:S(2)}) copy-start(bf16[1,197,768]{2,1,0:T(8,128)(2,1)} %param.11) | copy-start | bytes 907780
  374.9 11.9 %copy-start.27 = (bf16[1,197,12,64]{1,3,2,0:T(8,128)(2,1)S(1)}, bf16[1,197,12,64]{1,3,2,0:T(8,128)(2,1)}, u32[]{:S(2)}) copy-start(bf16[1,197,12,64]{1,3,2,0:T(8,128)(2,1)} %copy-done.26) | copy-start | bytes 907780
  374.9 11.9 %copy-start.32 = (bf16[12,64,197]{2,1,0:T(8,128)(2,1)S(1)}, bf16[12,64,197]{2,1,0:T(8,128)(2,1)}, u32[]{:S(2)}) copy-start(bf16[12,64,197]{2,1,0:T(8,128)(2,1)} %fusion.30) | copy-start | bytes 907780
  374.9 11.9 %copy-start.34 = (bf16[1,197,12,64]{1,3,2,0:T(8,128)(2,1)S(1)}, bf16[1,197,12,64]{1,3,2,0:T(8,128)(2,1)}, u32[]{:S(2)}) copy-start(bf16[1,197,12,64]{1,3,2,0:T(8,128)(2,1)} %get-tuple-element.109) | copy-start | bytes 907780
  391.5 297.2 %all-reduce.3.cloned.1.call-start = ((), (), s32[]{:S(2)}) async-start(), calls=%async_computation.8 | async-start | bytes 3538944 | tf_op jit(solution)/shard_map/psum | solution.py:282
  576.4 1.7 copy-start.3
  576.4 1.7 copy-start.10
  578.1 69.5 %copy-start.29 = (f32[12,96]{1,0:T(8,128)S(1)}, f32[12,96]{1,0:T(8,128)}, u32[]{:S(2)}) copy-start(f32[12,96]{1,0:T(8,128)} %param.18) | copy-start | bytes 13828
  578.1 69.5 %copy-start.30 = (f32[12,96]{1,0:T(8,128)S(1)}, f32[12,96]{1,0:T(8,128)}, u32[]{:S(2)}) copy-start(f32[12,96]{1,0:T(8,128)} %param.21) | copy-start | bytes 13828
  578.1 110.5 %copy-start = (f32[96,6144]{1,0:T(8,128)S(1)}, f32[96,6144]{1,0:T(8,128)}, u32[]{:S(2)}) copy-start(f32[96,6144]{1,0:T(8,128)} %param.13) | copy-start | bytes 7077892
  688.7 7.2 %copy-start.5 = (f32[384,768]{1,0:T(8,128)S(1)}, f32[384,768]{1,0:T(8,128)}, u32[]{:S(2)}) copy-start(f32[384,768]{1,0:T(8,128)} %param.14) | copy-start | bytes 3538948
  688.7 7.2 %copy-start.23 = (f32[384,768]{1,0:T(8,128)S(1)}, f32[384,768]{1,0:T(8,128)}, u32[]{:S(2)}) copy-start(f32[384,768]{1,0:T(8,128)} %param.17) | copy-start | bytes 3538948
  688.7 7.2 %copy-start.24 = (f32[384,768]{1,0:T(8,128)S(1)}, f32[384,768]{1,0:T(8,128)}, u32[]{:S(2)}) copy-start(f32[384,768]{1,0:T(8,128)} %param.20) | copy-start | bytes 3538948
  688.7 7.2 %copy-start.25 = (bf16[384,768]{1,0:T(8,128)(2,1)S(1)}, bf16[384,768]{1,0:T(8,128)(2,1)}, u32[]{:S(2)}) copy-start(bf16[384,768]{1,0:T(8,128)(2,1)} %get-tuple-element.87) | copy-start | bytes 1769476
Sparse Core Ops, SparseCore 0:
  10.7 140.2 all-gather.3
  153.8 77.4 all-gather.5
  234.9 176.1 reduce-scatter.7
  414.6 161.7 reduce-scatter.5
  580.0 61.0 reduce-scatter.9
  643.6 45.0 all-reduce.2
